TPU v7x, 32 devices: a whole 2x2x4 slice. The times are simulated.
32 devices in a mesh: groups: 2 (over x), facet: 16 (over z, y, core).
Axes of the slice: x: 2, y: 2, z: 4, core: 2. Of those that a mesh axis runs over, the one named last changes fastest.
Arguments:
- facets: bfloat16 [32, 2, 512, 512], P(('groups', 'facet')), parts along dimension 0, may hold values from -6 to 6
- facet_offsets: int32 [32, 2], P(('groups', 'facet')), parts along dimension 0, may hold values from 0 to 511
- subgrid_offsets: int32 [32, 2], P('groups'), parts along dimension 0, may hold values from 0 to 511
- w_terms: float32 [32], P(('groups', 'facet')), parts along dimension 0, may hold values from 2 to 16
- tile_count: int32 [32], P(('groups', 'facet')), parts along dimension 0, may hold values from 1 to 16, as said below
- tile_offsets: int32 [512, 2], P(('groups', 'facet')), parts along dimension 0, may hold values from 0 to 256
- observed: bfloat16 [512, 2, 128, 128], P(('groups', 'facet')), parts along dimension 0, may hold values from -6 to 6
Outputs:
- residual: bfloat16 [512, 2, 128, 128], P(('groups', 'facet')), parts along dimension 0
- facet_update: bfloat16 [32, 2, 512, 512], P(('groups', 'facet')), parts along dimension 0
There are 2 independent parts, one for each index of `groups`. A program takes and returns all parts, laid end to end along the dimension named above; each array names one. Nothing has to cross between parts.
Inputs may be any that keep to these rules, and one draw needn't show every extreme that they name: `tile_count`: live tile slots of each subgrid; some subgrid has all 16 slots live in every draw.
All inputs are finite; a program needn't handle non-finite values.
Results may differ from a plain program's by a relative error of at most 0.017.
Values may be sent and summed in bfloat16 or wider, within the bound.
A program may use at most 64 MiB of HBM per device.

v0:
```python
import math

import jax
import jax.numpy as jnp
from jax import lax
from jax.sharding import PartitionSpec as P

F = 512
M = 128
SG = 512
TV = 128


TWO_PI = 2.0 * math.pi


def basis_tables():
    index_f = jnp.arange(F, dtype=jnp.int32)
    product = index_f[:, None] * index_f[None, :] % F
    angle = -TWO_PI * product.astype(jnp.float32) / F
    scale = 1.0 / math.sqrt(F)
    return (
        (jnp.cos(angle) * scale).astype(jnp.bfloat16),
        (jnp.sin(angle) * scale).astype(jnp.bfloat16),
    )


def padding_tables(facet_count):
    rows = jnp.arange(SG, dtype=jnp.int32)
    columns = jnp.arange(M, dtype=jnp.int32)
    product = rows[:, None] * columns[None, :] % SG
    angle = TWO_PI * product.astype(jnp.float32) / SG
    scale = (M * math.sqrt(facet_count)) ** (-0.5)
    return (
        (jnp.cos(angle) * scale).astype(jnp.bfloat16),
        (jnp.sin(angle) * scale).astype(jnp.bfloat16),
    )


def taper_square():
    position = jnp.arange(M, dtype=jnp.float32)
    taper = 0.6 + 0.4 * jnp.sin(math.pi * (position + 0.5) / M)
    return taper[:, None] * taper[None, :]


def kernel_table():
    rows = jnp.arange(TV, dtype=jnp.float32)[:, None]
    columns = jnp.arange(2 * TV, dtype=jnp.float32)[None, :]
    distance = columns - 2.0 * rows - 1.0
    value = 0.75 * jnp.exp(-(distance / 1.5) * (distance / 1.5))
    return jnp.where(jnp.abs(distance) <= 4.0, value, jnp.zeros_like(value)).astype(jnp.bfloat16)


def facet_phase(offset):
    index_m = jnp.arange(M, dtype=jnp.int32)
    total = ((index_m * offset[0])[:, None] + (index_m * offset[1])[None, :]) % F
    angle = TWO_PI * total.astype(jnp.float32) / F
    return (jnp.cos(angle), jnp.sin(angle))


def screen_table(w_value):
    centred = jnp.arange(SG, dtype=jnp.float32) - SG / 2.0
    radius = (centred[:, None] * centred[:, None] + centred[None, :] * centred[None, :]) / (SG * SG)
    angle = TWO_PI * w_value * (jnp.sqrt(1.0 + radius) - 1.0)
    return (jnp.cos(angle), jnp.sin(angle))


def matmul(left, right):
    return jnp.dot(left, right, preferred_element_type=jnp.float32)


def complex_dot(left_real, left_imag, right_real, right_imag):
    real_part = matmul(left_real, right_real) - matmul(left_imag, right_imag)
    imag_part = matmul(left_real, right_imag) + matmul(left_imag, right_real)
    return (real_part, imag_part)


def facet_spectrum(facet, basis_real, basis_imag):
    half_real, half_imag = complex_dot(facet[0], facet[1], basis_real.T, basis_imag.T)
    return complex_dot(
        basis_real, basis_imag, half_real.astype(jnp.bfloat16), half_imag.astype(jnp.bfloat16)
    )


def extract(spectrum_real, spectrum_imag, offsets, phase_cos, phase_sin, taper2):
    stacked = jnp.stack([spectrum_real, spectrum_imag])
    padded = jnp.concatenate([stacked, stacked[:, :M, :]], axis=1)
    padded = jnp.concatenate([padded, padded[:, :, :M]], axis=2)
    zero = jnp.zeros((), jnp.int32)

    def window(offset):
        return lax.dynamic_slice(padded, (zero, offset[0], offset[1]), (2, M, M))

    windows = jax.vmap(window)(offsets)
    real_part = taper2 * (phase_cos * windows[:, 0] - phase_sin * windows[:, 1])
    imag_part = taper2 * (phase_cos * windows[:, 1] + phase_sin * windows[:, 0])
    return jnp.stack([real_part, imag_part], axis=1).astype(jnp.bfloat16)


def subgrid_model(summed, pad_real, pad_imag, screen_cos, screen_sin):
    inner_real, inner_imag = complex_dot(pad_real, pad_imag, summed[0], summed[1])
    image_real, image_imag = complex_dot(
        inner_real.astype(jnp.bfloat16), inner_imag.astype(jnp.bfloat16), pad_real.T, pad_imag.T
    )
    model_real = screen_cos * image_real - screen_sin * image_imag
    model_imag = screen_cos * image_imag + screen_sin * image_real
    return jnp.stack([model_real, model_imag]).astype(jnp.bfloat16)


def tile_terms(model, observed_tile, offset, kernel):
    zero = jnp.zeros((), jnp.int32)
    window = lax.dynamic_slice(model, (zero, offset[0], offset[1]), (2, 2 * TV, 2 * TV))
    left = jnp.einsum("jq,cqk->cjk", kernel, window, preferred_element_type=jnp.float32).astype(
        jnp.bfloat16
    )
    predicted = jnp.einsum("cjk,lk->cjl", left, kernel, preferred_element_type=jnp.float32)
    residual = (observed_tile.astype(jnp.float32) - predicted).astype(jnp.bfloat16)
    back = jnp.einsum("cjl,lk->cjk", residual, kernel, preferred_element_type=jnp.float32).astype(
        jnp.bfloat16
    )
    spread = jnp.einsum("jq,cjk->cqk", kernel, back, preferred_element_type=jnp.float32)
    return (residual, spread)


def add_window(adjoint, spread, offset):
    zero = jnp.zeros((), jnp.int32)
    start = (zero, offset[0], offset[1])
    current = lax.dynamic_slice(adjoint, start, spread.shape)
    return lax.dynamic_update_slice(adjoint, current + spread, start)


def back_coefficients(adjoint, pad_real, pad_imag, screen_cos, screen_sin):
    screened_real = (screen_cos * adjoint[0] + screen_sin * adjoint[1]).astype(jnp.bfloat16)
    screened_imag = (screen_cos * adjoint[1] - screen_sin * adjoint[0]).astype(jnp.bfloat16)
    reduced_real = (matmul(pad_real.T, screened_real) + matmul(pad_imag.T, screened_imag)).astype(
        jnp.bfloat16
    )
    reduced_imag = (matmul(pad_real.T, screened_imag) - matmul(pad_imag.T, screened_real)).astype(
        jnp.bfloat16
    )
    coef_real = matmul(reduced_real, pad_real) + matmul(reduced_imag, pad_imag)
    coef_imag = matmul(reduced_imag, pad_real) - matmul(reduced_real, pad_imag)
    return jnp.stack([coef_real, coef_imag]).astype(jnp.bfloat16)


def facet_back(back_spectrum, basis_real, basis_imag):
    half_real = (
        matmul(basis_real, back_spectrum[0]) + matmul(basis_imag, back_spectrum[1])
    ).astype(jnp.bfloat16)
    half_imag = (
        matmul(basis_real, back_spectrum[1]) - matmul(basis_imag, back_spectrum[0])
    ).astype(jnp.bfloat16)
    update_real = matmul(half_real, basis_real) + matmul(half_imag, basis_imag)
    update_imag = matmul(half_imag, basis_real) - matmul(half_real, basis_imag)
    return jnp.stack([update_real, update_imag]).astype(jnp.bfloat16)


def process_tiles(model, observed, tile_offsets, kernel, lower, upper):
    slots = observed.shape[0]

    def tile_step(slot, carry):
        residual_buf, adjoint = carry
        residual, spread = tile_terms(model, observed[slot], tile_offsets[slot], kernel)
        residual_buf = lax.dynamic_update_index_in_dim(residual_buf, residual, slot, 0)
        return (residual_buf, add_window(adjoint, spread, tile_offsets[slot]))

    start = (jnp.zeros((slots, 2, TV, TV), jnp.bfloat16), jnp.zeros((2, SG, SG), jnp.float32))
    return lax.fori_loop(lower, upper, tile_step, start)


def per_device(facets, facet_offsets, subgrid_offsets, w_terms, tile_count, tile_offsets, observed):
    facet_count = lax.axis_size("facet")
    basis_real, basis_imag = basis_tables()
    pad_real, pad_imag = padding_tables(facet_count)
    taper2 = taper_square()
    kernel = kernel_table()
    spectrum_real, spectrum_imag = facet_spectrum(facets[0], basis_real, basis_imag)
    phase_cos, phase_sin = facet_phase(facet_offsets[0])
    contributions = extract(
        spectrum_real, spectrum_imag, subgrid_offsets, phase_cos, phase_sin, taper2
    )
    summed = lax.psum_scatter(
        contributions.astype(jnp.float32), "facet", scatter_dimension=0, tiled=True
    )[0]
    screen_cos, screen_sin = screen_table(w_terms[0])
    model = subgrid_model(summed.astype(jnp.bfloat16), pad_real, pad_imag, screen_cos, screen_sin)
    count = tile_count[0]
    lowest = jnp.zeros((), jnp.int32)
    residual, adjoint = process_tiles(model, observed, tile_offsets, kernel, lowest, count)
    coefficient = back_coefficients(adjoint, pad_real, pad_imag, screen_cos, screen_sin)
    empty = jnp.zeros((2, F + M, F + M), jnp.float32)
    piece = lax.all_gather(coefficient[None], "facet", axis=0, tiled=True)

    def put(index, current):
        offset = subgrid_offsets[index]
        values = piece[index].astype(jnp.float32)
        values_real = taper2 * (phase_cos * values[0] + phase_sin * values[1])
        values_imag = taper2 * (phase_cos * values[1] - phase_sin * values[0])
        return add_window(current, jnp.stack([values_real, values_imag]), offset)

    buffer = lax.fori_loop(0, piece.shape[0], put, empty)
    folded = buffer[:, :F, :].at[:, :M, :].add(buffer[:, F:, :])
    folded = folded[:, :, :F].at[:, :, :M].add(folded[:, :, F:])
    update = facet_back(folded.astype(jnp.bfloat16), basis_real, basis_imag)
    return (residual, update[None])


def solution(mesh):
    placed = (
        P(("groups", "facet"), None, None, None),
        P(("groups", "facet"), None),
        P("groups", None),
        P(("groups", "facet")),
        P(("groups", "facet")),
        P(("groups", "facet"), None),
        P(("groups", "facet"), None, None, None),
    )
    return jax.shard_map(
        per_device,
        mesh=mesh,
        in_specs=placed,
        out_specs=(
            P(("groups", "facet"), None, None, None),
            P(("groups", "facet"), None, None, None),
        ),
        check_vma=False,
    )
```

profile of v0, /device:TPU:0, one launch (start us, length us, event | category | flops | bytes accessed | tf_op | source)
XLA Modules:
  0.0 676.9 jit_solution(7182427111298475314)
XLA Ops:
  7.2 5.1 fusion.99
  12.4 4.0 fusion.101
  16.4 4.4 fusion.69
  20.8 4.0 fusion.107
  24.7 4.6 fusion.68
  29.3 4.0 fusion.108
  33.3 4.1 fusion.66
  37.4 4.3 fusion.67
  42.4 42.2 %while.33 = (s32[]{:T(128)}, f32[2,640,640]{2,1,0:T(8,128)S(1)}, s32[16,3]{0,1:T(4,128)S(1)}, f32[16,2,128,128]{3,2,1,0:T(8,128)}, s32[]{:T(128)}) while((s32[]{:T(128)}, f32[2,640,640]{2,1,0:T(8,128)S(1)}, s32[16,3]{0,1:T(4,128)S(1)}, f32[16,2,128,128]{3,2,1,0:T(8,128)}, s32[]{:T(128)}) %tuple.101), condition=%wide.while_cond.2, body=%wide.while_body.2.sunk | while | flops 2 | bytes 263785 | solution.py:92
  64.1 2.0 bitcast_dynamic-update-slice_fusion.4
  74.6 2.0 bitcast_dynamic-update-slice_fusion.4
  77.3 2.0 bitcast_dynamic-update-slice_fusion.4
  91.1 63.7 %reduce-scatter.2.cloned.1.call-done = f32[1,2,128,128]{3,2,1,0:T(8,128)} async-done(((f32[16,2,128,128]{3,2,1,0:T(8,128)}), f32[1,2,128,128]{3,2,1,0:T(8,128)}) %reduce-scatter.2.cloned.1.call-update) | async-done | bytes 131088 | tf_op jit(solution)/shard_map/reduce_scatter | solution.py:182
  164.5 5.7 fusion.109
  172.7 51.2 %while.34 = (s32[]{:T(128)}, bf16[16,2,128,128]{3,2,1,0:T(8,128)(2,1)}, f32[2,512,512]{2,1,0:T(8,128)S(1)}, s32[]{:T(128)}, bf16[16,2,128,128]{3,2,1,0:T(8,128)(...) while((s32[]{:T(128)}, ...), condition=%wide.region_2.3_spmd.clone.clone, body=%wide.region_1.2_spmd.clone.clone.sunk | while | flops 102334472 | bytes 5768983 | solution.py:168
  177.8 2.1 bitcast_dynamic-update-slice_fusion.5
  181.0 8.5 %dynamic_update_slice.26 = f32[2,512,512]{2,1,0:T(8,128)S(1)} dynamic-update-slice(f32[2,512,512]{2,1,0:T(8,128)S(1)} %get-tuple-element.556, f32[2,256,256]{2,1,0:T(8,128)S(1)} %copy.19, s32[]{:T(128)} %constant.166.clone.1..sunk, s32[]{:T(128)S(6)} %select_n.283, s32[]{:T(128)S(6)} %select_n.284) | dynamic-update-slice | bytes 1048580 | tf_op jit(solution)/shard_map/while/body/dynamic_update_slice | solution.py:129
  194.6 2.1 bitcast_dynamic-update-slice_fusion.5
  197.9 9.6 %dynamic_update_slice.26 = f32[2,512,512]{2,1,0:T(8,128)S(1)} dynamic-update-slice(f32[2,512,512]{2,1,0:T(8,128)S(1)} %get-tuple-element.556, f32[2,256,256]{2,1,0:T(8,128)S(1)} %copy.19, s32[]{:T(128)} %constant.166.clone.1..sunk, s32[]{:T(128)S(6)} %select_n.283, s32[]{:T(128)S(6)} %select_n.284) | dynamic-update-slice | bytes 1048580 | tf_op jit(solution)/shard_map/while/body/dynamic_update_slice | solution.py:129
  212.6 2.1 bitcast_dynamic-update-slice_fusion.5
  215.8 7.5 %dynamic_update_slice.26 = f32[2,512,512]{2,1,0:T(8,128)S(1)} dynamic-update-slice(f32[2,512,512]{2,1,0:T(8,128)S(1)} %get-tuple-element.556, f32[2,256,256]{2,1,0:T(8,128)S(1)} %copy.19, s32[]{:T(128)} %constant.166.clone.1..sunk, s32[]{:T(128)S(6)} %select_n.283, s32[]{:T(128)S(6)} %select_n.284) | dynamic-update-slice | bytes 1048580 | tf_op jit(solution)/shard_map/while/body/dynamic_update_slice | solution.py:129
  223.9 5.4 fusion.88
  239.4 260.1 %all-gather.2.cloned.1.call-done = bf16[16,2,128,128]{3,2,1,0:T(8,128)(2,1)} async-done(((bf16[1,2,128,128]{3,2,1,0:T(8,128)(2,1)}), bf16[16,2,128,128]{3,2,1,0:T(8,128)(2,1)}) %all-gather.2.cloned.1.call-update) | async-done | bytes 1048592 | tf_op jit(solution)/shard_map/all_gather | solution.py:192
  499.7 132.2 %while.35 = (s32[]{:T(128)}, f32[2,640,640]{2,1,0:T(8,128)S(1)}, s32[16,2]{0,1:T(2,128)S(1)}, bf16[16,2,128,128]{3,2,1,0:T(8,128)(2,1)}, f32[128]{0:T(128)S(1)},...) while((s32[]{:T(128)}, f32[2,640,640]{2,1,0:T(8,128)S(1)}, ...), condition=%wide.region_4.5_spmd.clone.clone.clone, body=%wide.region_3.4_spmd.clone.clone.clone.sunk | while | flops 475144 | bytes 1116381 | solution.py:201
  505.5 2.5 dynamic_update_slice.27
  513.8 2.5 dynamic_update_slice.27
  522.2 2.5 dynamic_update_slice.27
  530.5 2.5 dynamic_update_slice.27
  538.8 2.1 dynamic_update_slice.27
  546.7 2.5 dynamic_update_slice.27
  555.0 2.4 dynamic_update_slice.27
  563.2 2.4 dynamic_update_slice.27
  571.4 2.5 dynamic_update_slice.27
  579.7 2.5 dynamic_update_slice.27
  588.0 2.1 dynamic_update_slice.27
  596.0 2.5 dynamic_update_slice.27
  604.3 2.5 dynamic_update_slice.27
  612.6 2.5 dynamic_update_slice.27
  621.0 2.5 dynamic_update_slice.27
  629.3 2.5 dynamic_update_slice.27
  632.4 4.0 fusion.106
  636.4 4.0 fusion.104
  640.4 4.2 fusion.70
  644.6 5.0 fusion.105
  649.6 4.2 fusion.71
  653.8 4.8 fusion.103
  658.7 5.0 fusion.75
  663.7 5.0 fusion.74
  (196 shorter events, 102.8 us)
Async XLA Ops:
  7.2 5.2 copy-start.3
  7.2 147.6 %reduce-scatter.2.cloned.1.call-start = ((), (), s32[]{:S(2)}) async-start(), calls=%async_computation.1 | async-start | bytes 2228224 | tf_op jit(solution)/shard_map/reduce_scatter | solution.py:182
  41.7 0.7 copy-start
  41.7 42.9 %copy-start.2 = (s32[1,2]{1,0:T(1,128)S(1)}, s32[1,2]{1,0:T(1,128)}, u32[]{:S(2)}) copy-start(s32[1,2]{1,0:T(1,128)} %param.16) | copy-start | bytes 28
  90.3 409.2 %all-gather.2.cloned.1.call-start = ((), (), s32[]{:S(2)}) async-start(), calls=%async_computation.2 | async-start | bytes 1114112 | tf_op jit(solution)/shard_map/all_gather | solution.py:192
  170.2 2.5 copy-start.1
Sparse Core Ops, SparseCore 0:
  90.4 64.2 reduce-scatter.1
  239.6 259.8 all-gather.1
where the time goes:
time: 684 us; the launch traced here: 677 us
  waiting for transfers between devices  324 us (47%)
  local copies, waits for them, and re-layouts  123 us (18%)
  matrix products  102 us (15%)
  loops' own time  76.4 us (11%)
  other arithmetic  36 us (5%)
  between operations  15.2 us (2%)
    all_gather x1, waiting for transfers between devices, per_device(): piece = lax.all_gather(coefficient[None], 'facet', axis=0, tiled=True)  260 us
    dot_general x32, matrix products, matmul(): return jnp.dot(left, right, preferred_element_type=jnp.float32)  94.4 us
    dynamic_update_slice x22, local copies, waits for them, and re-layouts, add_window(): return lax.dynamic_update_slice(adjoint, current + spread, start)  65.1 us
    reduce_scatter x1, waiting for transfers between devices, per_device(): lax.psum_scatter(contributions.astype(jnp.float32), 'facet', scatter_dime...  63.7 us
    another operation x1, loops' own time, per_device(): buffer = lax.fori_loop(0, piece.shape[0], put, empty)  62.4 us
    gather x48, local copies, waits for them, and re-layouts  42.2 us
    another operation x1, loops' own time, process_tiles(): return lax.fori_loop(lower, upper, tile_step, start)  14 us
    convert_element_type x16, other arithmetic, put(): values = piece[index].astype(jnp.float32)  13.7 us
  transfers between devices with their start and end apart: 2, of which 2 were waited for; matrix products, arithmetic and copies ran while one was open for 0% of the time, Pallas kernels for 0%

commit v1 on v0

v1 whole, which is shorter than its diff:
```python
import functools
import math

import jax
import jax.numpy as jnp
import ml_dtypes
import numpy as np
from jax import lax
from jax.experimental import pallas as pl
from jax.experimental.pallas import tpu as pltpu
from jax.sharding import PartitionSpec as P

F = 512
M = 128
SG = 512
TV = 128
SPAN = 384
WIDE = F + M

BF16 = jnp.bfloat16
F32 = jnp.float32
TWO_PI = 2.0 * math.pi
MESH = pl.DeviceIdType.MESH
VMEM = pltpu.VMEM
LIMIT = 48 * 1024 * 1024


def basis_table():
    index = np.arange(F)
    angle = -TWO_PI * (index[:, None] * index[None, :] % F) / F
    scale = 1.0 / math.sqrt(F)
    return np.stack([np.cos(angle) * scale, np.sin(angle) * scale]).astype(ml_dtypes.bfloat16)


def padding_table(facet_count):
    angle = TWO_PI * (np.arange(SG)[:, None] * np.arange(M)[None, :] % SG) / SG
    scale = (M * math.sqrt(facet_count)) ** (-0.5)
    return np.stack([np.cos(angle) * scale, np.sin(angle) * scale]).astype(ml_dtypes.bfloat16)


def taper_square():
    taper = 0.6 + 0.4 * np.sin(math.pi * (np.arange(M) + 0.5) / M)
    return (taper[:, None] * taper[None, :]).astype(np.float32)


def kernel_table():
    distance = np.arange(2 * TV)[None, :] - 2.0 * np.arange(TV)[:, None] - 1.0
    value = 0.75 * np.exp(-(distance / 1.5) * (distance / 1.5))
    return np.where(np.abs(distance) <= 4.0, value, 0.0).astype(ml_dtypes.bfloat16).astype(np.float32)


def dot(left, right):
    return jnp.dot(left, right, preferred_element_type=F32)


def dot_t(left, right):
    return lax.dot_general(left, right, (((1,), (1,)), ((), ())), preferred_element_type=F32)


def cos_sin_turns(turns):
    quarter = jnp.floor(turns * 4.0 + 0.5)
    y = (turns - quarter * 0.25) * TWO_PI
    y2 = y * y
    sine = y * (1.0 + y2 * (-1.0 / 6 + y2 * (1.0 / 120 + y2 * (-1.0 / 5040 + y2 * (1.0 / 362880)))))
    cosine = 1.0 + y2 * (
        -0.5 + y2 * (1.0 / 24 + y2 * (-1.0 / 720 + y2 * (1.0 / 40320 - y2 * (1.0 / 3628800))))
    )
    which = quarter.astype(jnp.int32) & 3
    odd = (which & 1) == 1
    first = jnp.where(odd, sine, cosine)
    second = jnp.where(odd, cosine, sine)
    cos_value = jnp.where((which == 1) | (which == 2), -first, first)
    sin_value = jnp.where(which >= 2, -second, second)
    return cos_value, sin_value


def tapered_phase(offset_ref, taper_ref):
    rows = lax.broadcasted_iota(jnp.int32, (M, M), 0)
    columns = lax.broadcasted_iota(jnp.int32, (M, M), 1)
    total = (rows * offset_ref[0, 0] + columns * offset_ref[0, 1]) & (F - 1)
    cos_value, sin_value = cos_sin_turns(total.astype(F32) * (1.0 / F))
    taper = taper_ref[...]
    return cos_value * taper, sin_value * taper


def forward_kernel(n, foff, soff, facet, basis, taper, out, half, spec, phase):
    phase[0], phase[1] = tapered_phase(foff, taper)
    lanes = lax.broadcasted_iota(jnp.int32, (M, M), 1)

    @pl.loop(0, 2)
    def _(c):
        cols = pl.ds(pl.multiple_of(c * 256, 256), 256)
        br, bi = basis[0, :, cols], basis[1, :, cols]
        half[0, :, cols] = (dot(facet[0], br) - dot(facet[1], bi)).astype(BF16)
        half[1, :, cols] = (dot(facet[0], bi) + dot(facet[1], br)).astype(BF16)

    @pl.loop(0, 2)
    def _(c):
        cols = pl.ds(pl.multiple_of(c * 256, 256), 256)
        hr, hi = half[0, :, cols], half[1, :, cols]
        real = dot(basis[0], hr) - dot(basis[1], hi)
        imag = dot(basis[0], hi) + dot(basis[1], hr)
        for side in range(2):
            part = slice(side * M, side * M + M)
            spec[0, c * 2 + side, 0:F] = real[:, part]
            spec[1, c * 2 + side, 0:F] = imag[:, part]

    spec[:, 0 : F // M, F:WIDE] = spec[:, 0 : F // M, 0:M]
    spec[:, F // M] = spec[:, 0]

    @pl.loop(0, n)
    def _(s):
        sx, sy = soff[s, 0], soff[s, 1]
        tile, offset = sy >> 7, sy & 127
        shift = (M - offset) & 127
        kept = lanes < M - offset
        rows = pl.ds(sx, M)

        def window(plane):
            low = pltpu.roll(spec[plane, tile, rows], shift, 1)
            high = pltpu.roll(spec[plane, tile + 1, rows], shift, 1)
            return jnp.where(kept, low, high)

        real, imag = window(0), window(1)
        pc, ps = phase[0], phase[1]
        out[s & 1, s >> 1, 0] = (pc * real - ps * imag).astype(BF16)
        out[s & 1, s >> 1, 1] = (pc * imag + ps * real).astype(BF16)


def greet(me, chips, core):
    barrier = pltpu.get_barrier_semaphore()
    chip = me // 2
    for k in range(1, chips):
        pl.semaphore_signal(
            barrier, inc=1, device_id={"facet": lax.rem(chip + k, chips) * 2 + core}, device_id_type=MESH
        )
    pl.semaphore_signal(barrier, inc=1, device_id={"facet": chip * 2 + 1 - core}, device_id_type=MESH)
    pl.semaphore_wait(barrier, chips)


def reduce_kernel(chips, contrib, summed, near, pair, far, near_s, near_r, far_s, far_r):
    me = lax.axis_index("facet")
    chip, core = me // 2, lax.rem(me, 2)
    sibling = chip * 2 + 1 - core
    greet(me, chips, core)

    def near_copy(k):
        j = lax.rem(chip + k, chips)
        return pltpu.make_async_remote_copy(
            src_ref=contrib.at[1 - core, j],
            dst_ref=near.at[j],
            send_sem=near_s.at[j],
            recv_sem=near_r.at[j],
            device_id={"facet": sibling},
            device_id_type=MESH,
        )

    def far_send(k):
        j = lax.rem(chip + k, chips)
        return pltpu.make_async_remote_copy(
            src_ref=pair.at[j],
            dst_ref=far.at[chip],
            send_sem=far_s.at[j],
            recv_sem=far_r.at[chip],
            device_id={"facet": j * 2 + core},
            device_id_type=MESH,
        )

    def far_arrival(j):
        return pltpu.make_async_remote_copy(
            src_ref=pair.at[j],
            dst_ref=far.at[j],
            send_sem=far_s.at[j],
            recv_sem=far_r.at[j],
            device_id={"facet": j * 2 + core},
            device_id_type=MESH,
        )

    order = list(range(1, chips)) + [0]

    @pl.loop(1, chips + 1)
    def _(k):
        near_copy(k).start()

    @pl.loop(1, chips)
    def _(k):
        near_copy(k).wait_recv()
        j = lax.rem(chip + k, chips)
        pair[j] = (contrib[core, j].astype(F32) + near[j].astype(F32)).astype(BF16)
        far_send(k).start()

    near_copy(chips).wait_recv()
    summed[...] = contrib[core, chip].astype(F32) + near[chip].astype(F32)

    @pl.loop(1, chips)
    def _(k):
        j = lax.rem(chip + k, chips)
        far_arrival(j).wait_recv()
        summed[...] += far[j].astype(F32)

    @pl.loop(1, chips)
    def _(k):
        far_send(k).wait_send()

    @pl.loop(1, chips + 1)
    def _(k):
        near_copy(k).wait_send()


def gather_kernel(chips, mine, out, far_s, far_r, near_s, near_r, local):
    me = lax.axis_index("facet")
    chip, core = me // 2, lax.rem(me, 2)
    sibling = chip * 2 + 1 - core
    greet(me, chips, core)

    def far_send(k):
        j = lax.rem(chip + k, chips)
        return pltpu.make_async_remote_copy(
            src_ref=mine,
            dst_ref=out.at[me],
            send_sem=far_s.at[j],
            recv_sem=far_r.at[chip],
            device_id={"facet": j * 2 + core},
            device_id_type=MESH,
        )

    def far_arrival(j):
        return pltpu.make_async_remote_copy(
            src_ref=mine,
            dst_ref=out.at[j * 2 + core],
            send_sem=far_s.at[j],
            recv_sem=far_r.at[j],
            device_id={"facet": j * 2 + core},
            device_id_type=MESH,
        )

    def near_send(j):
        return pltpu.make_async_remote_copy(
            src_ref=out.at[j * 2 + core],
            dst_ref=out.at[j * 2 + core],
            send_sem=near_s.at[j],
            recv_sem=near_r.at[j],
            device_id={"facet": sibling},
            device_id_type=MESH,
        )

    def near_first():
        return pltpu.make_async_remote_copy(
            src_ref=mine,
            dst_ref=out.at[me],
            send_sem=near_s.at[chip],
            recv_sem=near_r.at[chip],
            device_id={"facet": sibling},
            device_id_type=MESH,
        )

    def near_arrival(j):
        return pltpu.make_async_remote_copy(
            src_ref=out.at[j * 2 + 1 - core],
            dst_ref=out.at[j * 2 + 1 - core],
            send_sem=near_s.at[j],
            recv_sem=near_r.at[j],
            device_id={"facet": sibling},
            device_id_type=MESH,
        )

    @pl.loop(1, chips)
    def _(k):
        far_send(k).start()

    near_first().start()
    own = pltpu.make_async_copy(mine, out.at[me], local)
    own.start()

    @pl.loop(1, chips)
    def _(k):
        j = lax.rem(chip + chips - k, chips)
        far_arrival(j).wait_recv()
        near_send(j).start()

    @pl.loop(0, chips)
    def _(k):
        near_arrival(lax.rem(chip + k, chips)).wait_recv()

    @pl.loop(1, chips)
    def _(k):
        far_send(k).wait_send()
        near_send(lax.rem(chip + k, chips)).wait_send()

    near_first().wait_send()
    own.wait()


def subgrid_kernel(
    slots, w_ref, count_ref, toff, summed, pad, pad_t, ker, ker_t, observed,
    residual, coefficient, inner, screen, model, adjoint, reduced, wide_t
):
    adjoint[...] = jnp.zeros_like(adjoint)
    residual[...] = jnp.zeros_like(residual)
    wide_t[...] = ker_t[...]
    sr, si = summed[0].astype(BF16), summed[1].astype(BF16)
    inner[0] = (dot(pad[0], sr) - dot(pad[1], si)).astype(BF16)
    inner[1] = (dot(pad[0], si) + dot(pad[1], sr)).astype(BF16)
    w_value = w_ref[0]

    @pl.loop(0, 4)
    def _(c):
        rows = pl.ds(pl.multiple_of(c * 128, 128), 128)
        u = (lax.broadcasted_iota(jnp.int32, (128, SG), 0) + (c * 128 - 256)).astype(F32)
        v = (lax.broadcasted_iota(jnp.int32, (128, SG), 1) - 256).astype(F32)
        radius = (u * u + v * v) * (1.0 / (SG * SG))
        cos_value, sin_value = cos_sin_turns(w_value * (jnp.sqrt(1.0 + radius) - 1.0))
        screen[0, rows, :] = cos_value
        screen[1, rows, :] = sin_value
        ir, ii = inner[0, rows, :], inner[1, rows, :]
        image_real = dot(ir, pad_t[0]) - dot(ii, pad_t[1])
        image_imag = dot(ir, pad_t[1]) + dot(ii, pad_t[0])
        model[0, rows, :] = (cos_value * image_real - sin_value * image_imag).astype(BF16)
        model[1, rows, :] = (cos_value * image_imag + sin_value * image_real).astype(BF16)

    count = count_ref[0]

    @pl.loop(0, count)
    def _(t):
        ou, ov = toff[t, 0], toff[t, 1]
        u0 = pl.multiple_of(jnp.minimum(ou & ~127, 128), 128)
        v0 = pl.multiple_of(jnp.minimum(ov & ~127, 128), 128)
        du, dv = ou - u0, ov - v0
        rows, cols = pl.ds(u0, SPAN), pl.ds(v0, SPAN)
        table = ker[...]
        ku = pltpu.roll(table, du, 1).astype(BF16)
        kv = pltpu.roll(table, dv, 1).astype(BF16)
        kut = wide_t[pl.ds(128 - du, SPAN), :].astype(BF16)
        left = jnp.concatenate(
            [dot(ku, model[0, rows, cols]).astype(BF16), dot(ku, model[1, rows, cols]).astype(BF16)], axis=0
        )
        predicted = dot_t(left, kv)
        seen = observed[t].reshape(2 * TV, TV).astype(F32)
        rest = (seen - predicted).astype(BF16)
        residual[t] = rest.reshape(2, TV, TV)
        back = dot(rest, kv).astype(BF16)
        adjoint[0, rows, cols] += dot(kut, back[:TV])
        adjoint[1, rows, cols] += dot(kut, back[TV:])

    reduced[...] = jnp.zeros_like(reduced)

    @pl.loop(0, 2)
    def _(c):
        cols = pl.ds(pl.multiple_of(c * 256, 256), 256)
        ar, ai = adjoint[0, :, cols], adjoint[1, :, cols]
        sc, ss = screen[0, :, cols], screen[1, :, cols]
        xr = (sc * ar + ss * ai).astype(BF16)
        xi = (sc * ai - ss * ar).astype(BF16)
        reduced[0, :, cols] = (dot(pad_t[0], xr) + dot(pad_t[1], xi)).astype(BF16)
        reduced[1, :, cols] = (dot(pad_t[0], xi) - dot(pad_t[1], xr)).astype(BF16)

    rr, ri = reduced[0], reduced[1]
    coefficient[0] = (dot(rr, pad[0]) + dot(ri, pad[1])).astype(BF16)
    coefficient[1] = (dot(ri, pad[0]) - dot(rr, pad[1])).astype(BF16)


def backward_kernel(n, foff, soff, piece, basis, taper, out, acc, spec, half, phase):
    phase[0], phase[1] = tapered_phase(foff, taper)
    lanes = lax.broadcasted_iota(jnp.int32, (M, M), 1)
    acc[...] = jnp.zeros_like(acc)

    @pl.loop(0, n)
    def _(s):
        sx, sy = soff[s, 0], soff[s, 1]
        tile, shift = sy >> 7, sy & 127
        rows = pl.ds(sx, M)
        kept = lanes >= shift
        pc, ps = phase[0], phase[1]
        real, imag = piece[s, 0].astype(F32), piece[s, 1].astype(F32)
        blank = jnp.zeros((M, M), F32)
        values = (pc * real + ps * imag, pc * imag - ps * real)
        for plane in range(2):
            turned = pltpu.roll(values[plane], shift, 1)
            acc[plane, tile, rows] += jnp.where(kept, turned, blank)
            acc[plane, tile + 1, rows] += jnp.where(kept, blank, turned)

    acc[:, 0] += acc[:, F // M]
    acc[:, 0 : F // M, 0:M] += acc[:, 0 : F // M, F:WIDE]
    for k in range(F // M):
        spec[:, :, k * M : k * M + M] = acc[:, k, 0:F].astype(BF16)

    @pl.loop(0, 2)
    def _(c):
        cols = pl.ds(pl.multiple_of(c * 256, 256), 256)
        xr, xi = spec[0, :, cols], spec[1, :, cols]
        half[0, :, cols] = (dot(basis[0], xr) + dot(basis[1], xi)).astype(BF16)
        half[1, :, cols] = (dot(basis[0], xi) - dot(basis[1], xr)).astype(BF16)

    @pl.loop(0, 2)
    def _(c):
        cols = pl.ds(pl.multiple_of(c * 256, 256), 256)
        br, bi = basis[0, :, cols], basis[1, :, cols]
        out[0, :, cols] = (dot(half[0], br) + dot(half[1], bi)).astype(BF16)
        out[1, :, cols] = (dot(half[1], br) - dot(half[0], bi)).astype(BF16)


SMEM_SPEC = pl.BlockSpec(memory_space=pltpu.SMEM)
VMEM_SPEC = pl.BlockSpec(memory_space=pltpu.VMEM)
DMA = pltpu.SemaphoreType.DMA


def per_device(facets, facet_offsets, subgrid_offsets, w_terms, tile_count, tile_offsets, observed):
    n = lax.axis_size("facet")
    chips = n // 2
    slots = observed.shape[0]
    basis = jnp.asarray(basis_table())
    pad_np = padding_table(n)
    pad = jnp.asarray(pad_np)
    pad_t = jnp.asarray(np.ascontiguousarray(pad_np.transpose(0, 2, 1)))
    taper = jnp.asarray(taper_square())
    table = kernel_table()
    ker_np = np.zeros((TV, SPAN), np.float32)
    ker_np[:, : 2 * TV] = table
    ker_t_np = np.zeros((4 * TV, TV), np.float32)
    ker_t_np[TV : 3 * TV] = table.T
    plain = pltpu.CompilerParams(vmem_limit_bytes=LIMIT)

    contrib = pl.pallas_call(
        functools.partial(forward_kernel, n),
        out_shape=jax.ShapeDtypeStruct((2, chips, 2, M, M), BF16),
        in_specs=[SMEM_SPEC, SMEM_SPEC, VMEM_SPEC, VMEM_SPEC, VMEM_SPEC],
        out_specs=VMEM_SPEC,
        scratch_shapes=[
            VMEM((2, F, F), BF16), VMEM((2, WIDE // M, WIDE, M), F32), VMEM((2, M, M), F32),
        ],
        compiler_params=plain,
        name="forward",
    )(facet_offsets, subgrid_offsets, facets[0], basis, taper)

    summed = pl.pallas_call(
        functools.partial(reduce_kernel, chips),
        out_shape=jax.ShapeDtypeStruct((2, M, M), F32),
        in_specs=[VMEM_SPEC],
        out_specs=VMEM_SPEC,
        scratch_shapes=[VMEM((chips, 2, M, M), BF16)] * 3 + [DMA((chips,))] * 4,
        compiler_params=pltpu.CompilerParams(
            vmem_limit_bytes=LIMIT, collective_id=0, has_side_effects=True
        ),
        name="reduce",
    )(contrib)

    residual, coefficient = pl.pallas_call(
        functools.partial(subgrid_kernel, slots),
        out_shape=(
            jax.ShapeDtypeStruct((slots, 2, TV, TV), BF16),
            jax.ShapeDtypeStruct((2, M, M), BF16),
        ),
        in_specs=[SMEM_SPEC] * 3 + [VMEM_SPEC] * 6,
        out_specs=(VMEM_SPEC, VMEM_SPEC),
        scratch_shapes=[
            VMEM((2, SG, M), BF16), VMEM((2, SG, SG), F32), VMEM((2, SG, SG), BF16),
            VMEM((2, SG, SG), F32), VMEM((2, M, SG), BF16), VMEM((4 * TV, TV), F32),
        ],
        compiler_params=plain,
        name="subgrid",
    )(
        w_terms, tile_count, tile_offsets, summed, pad, pad_t,
        jnp.asarray(ker_np), jnp.asarray(ker_t_np), observed,
    )

    piece = pl.pallas_call(
        functools.partial(gather_kernel, chips),
        out_shape=jax.ShapeDtypeStruct((n, 2, M, M), BF16),
        in_specs=[VMEM_SPEC],
        out_specs=VMEM_SPEC,
        scratch_shapes=[DMA((chips,))] * 4 + [DMA],
        compiler_params=pltpu.CompilerParams(
            vmem_limit_bytes=LIMIT, collective_id=1, has_side_effects=True
        ),
        name="gather",
    )(coefficient)

    update = pl.pallas_call(
        functools.partial(backward_kernel, n),
        out_shape=jax.ShapeDtypeStruct((2, F, F), BF16),
        in_specs=[SMEM_SPEC, SMEM_SPEC, VMEM_SPEC, VMEM_SPEC, VMEM_SPEC],
        out_specs=VMEM_SPEC,
        scratch_shapes=[
            VMEM((2, WIDE // M, WIDE, M), F32), VMEM((2, F, F), BF16), VMEM((2, F, F), BF16),
            VMEM((2, M, M), F32),
        ],
        compiler_params=plain,
        name="backward",
    )(facet_offsets, subgrid_offsets, piece, basis, taper)
    return (residual, update[None])


def solution(mesh):
    placed = (
        P(("groups", "facet"), None, None, None),
        P(("groups", "facet"), None),
        P("groups", None),
        P(("groups", "facet")),
        P(("groups", "facet")),
        P(("groups", "facet"), None),
        P(("groups", "facet"), None, None, None),
    )
    return jax.shard_map(
        per_device,
        mesh=mesh,
        in_specs=placed,
        out_specs=(
            P(("groups", "facet"), None, None, None),
            P(("groups", "facet"), None, None, None),
        ),
        check_vma=False,
    )
```

time: 684 us -> 71.5 us (0.10)
  waiting for transfers between devices: 324 us -> 0 us
  local copies, waits for them, and re-layouts: 123 us -> 5.32 us
  matrix products: 102 us -> 0 us
  loops' own time: 76.4 us -> 0 us
  Pallas kernels: 0 us -> 63.3 us
  other arithmetic: 36 us -> 0 us
  between operations: 15.2 us -> 2.03 us
    all_gather x1 -> x0, waiting for transfers between devices: 260 us -> none  [per_device(): piece = lax.all_gather(coefficient[None], 'facet', axis=0, tiled=True)]
    dot_general x38 -> x0, matrix products: 102 us -> none  [the longest x32 94.4 us: matmul(): return jnp.dot(left, right, preferred_element_type=jnp.float32)]
    another operation x3 -> x0, loops' own time: 76.4 us -> none  [the longest x1 62.4 us: per_device(): buffer = lax.fori_loop(0, piece.shape[0], put, empty)]
    dynamic_update_slice x22 -> x0, local copies, waits for them, and re-layouts: 65.1 us -> none  [add_window(): return lax.dynamic_update_slice(adjoint, current + spread, start)]
    reduce_scatter x1 -> x0, waiting for transfers between devices: 63.7 us -> none  [per_device(): lax.psum_scatter(contributions.astype(jnp.float32), 'facet', scatter_dime...]
    pallas_call x0 -> x5, Pallas kernels: none -> 63.3 us  [the longest x1 27.3 us: per_device(): pl.pallas_call(functools.partial(gather_kernel, chips), out_shape=jax.Sha...]
    gather x48 -> x0, local copies, waits for them, and re-layouts: 42.2 us -> none
    convert_element_type x19 -> x0, other arithmetic: 21.5 us -> none  [the longest x16 13.7 us: put(): values = piece[index].astype(jnp.float32)]
  transfers between devices with their start and end apart: 2 -> 0, of which waited for: 2 -> 0; matrix products, arithmetic and copies ran while one was open for 0% -> 0% of each run, Pallas kernels for 0% -> 0%
where the time goes in v1:
time: 71.5 us; the launch traced here: 70.7 us
  Pallas kernels  63.3 us (89%)
  local copies, waits for them, and re-layouts  5.32 us (7%)
  between operations  2.03 us (3%)
    pallas_call x1, Pallas kernels, per_device(): pl.pallas_call(functools.partial(gather_kernel, chips), out_shape=jax.Sha...  27.3 us
    pallas_call x1, Pallas kernels, per_device(): pl.pallas_call(functools.partial(reduce_kernel, chips), out_shape=jax.Sha...  16.2 us
    pallas_call x1, Pallas kernels, per_device(): pl.pallas_call(functools.partial(subgrid_kernel, slots), out_shape=(jax.S...  7.02 us
    pallas_call x1, Pallas kernels, per_device(): pl.pallas_call(functools.partial(backward_kernel, n), out_shape=jax.Shape...  6.83 us
    pallas_call x1, Pallas kernels, per_device(): pl.pallas_call(functools.partial(forward_kernel, n), out_shape=jax.ShapeD...  5.96 us
    unnamed x28, local copies, waits for them, and re-layouts  5.32 us

profile of v1, /device:TPU:0, one launch (start us, length us, event | category | flops | bytes accessed | tf_op | source)
XLA Modules:
  0.0 70.7 jit_solution(10901618026124465775)
XLA Ops:
  1.9 0.0 copy-start.11
  1.9 0.7 copy-done.11
  2.6 0.0 copy-start.12
  2.6 0.1 copy.15.soff
  2.7 0.6 copy-done.12
  3.3 0.0 copy-start.10
  3.3 0.1 copy.16.toff
  3.4 0.6 copy-done.10
  3.9 0.0 copy-start
  3.9 1.2 %copy-done = bf16[2,512,512]{2,1,0:T(8,128)(2,1)S(1)} copy-done((bf16[2,512,512]{2,1,0:T(8,128)(2,1)S(1)}, bf16[2,512,512]{2,1,0:T(8,128)(2,1)}, u32[]{:S(2)}) %copy-start) | copy-done | bytes 1048600
  5.2 0.0 copy-start.2
  5.2 1.2 %copy-done.2 = bf16[1,2,512,512]{3,2,1,0:T(8,128)(2,1)S(1)} copy-done((bf16[1,2,512,512]{3,2,1,0:T(8,128)(2,1)S(1)}, bf16[1,2,512,512]{3,2,1,0:T(8,128)(2,1)}, u32[]{:S(2)}) %copy-start.2) | copy-done | bytes 1048600
  6.4 0.0 copy-start.4
  6.4 0.8 %copy-done.4 = f32[128,128]{1,0:T(8,128)S(1)} copy-done((f32[128,128]{1,0:T(8,128)S(1)}, f32[128,128]{1,0:T(8,128)}, u32[]{:S(2)}) %copy-start.4) | copy-done | bytes 65560
  7.2 0.0 copy-start.6
  7.2 0.0 copy-start.7
  7.2 0.0 copy-start.8
  7.2 0.0 copy-start.9
  7.2 6.0 %forward.1.contrib = bf16[2,8,2,128,128]{4,3,2,1,0:T(8,128)(2,1)S(1)} custom-call(s32[1,2]{1,0:T(1,128)S(1)} %copy-done.10, s32[16,2]{1,0:T(8,128)S(1)} %copy.15.soff, bf16[2,512,512]{2,1,0:T(8,128)(2,1)S(1)} %bitcast.2, bf16[2,512,512]{2,1,0:T(8,128)(2,1)S(1)} %copy-done, f32[128,128]{1,0:T(8,128)S(1)} %copy-done.4), custom_call_target="tpu_custom_call" | custom-call | tf_op jit(solution)/shard_map/forward/pallas_call | solution.py:423
  13.2 0.0 copy-start.3
  13.2 16.2 %reduce.1.summed = f32[2,128,128]{2,1,0:T(8,128)S(1)} custom-call(bf16[2,8,2,128,128]{4,3,2,1,0:T(8,128)(2,1)S(1)} %forward.1.contrib), custom_call_target="tpu_custom_call" | custom-call | tf_op jit(solution)/shard_map/reduce/pallas_call | solution.py:435
  29.4 0.0 copy-done.6
  29.4 0.0 copy-done.7
  29.4 0.0 copy-done.8
  29.4 0.0 copy-done.9
  29.5 0.0 copy-done.3
  29.5 7.0 %subgrid.1 = (bf16[16,2,128,128]{3,2,1,0:T(8,128)(2,1)}, bf16[2,128,128]{2,1,0:T(8,128)(2,1)S(1)}) custom-call(f32[1]{0:T(128)S(6)} %copy.18.w_ref, s32[1]{0:T(128)S(6)} %copy.19.count_ref, s32[16,2]{1,0:T(8,128)S(1)} %copy.16.toff, f32[2,128,128]{2,1,0:T(8,128)S(1)} %reduce.1.summed, bf16[2,512,128]{2,1,0:T(8,128)(2,1)S(1)} %copy-done.8, ...), custom_call_target="tpu_custom_call" | custom-call | tf_op jit(solution)/shard_map/subgrid/pallas_call | solution.py:447
  36.5 0.0 copy-start.1
  36.5 0.0 copy-start.5
  36.5 27.3 %gather.1.piece = bf16[16,2,128,128]{3,2,1,0:T(8,128)(2,1)S(1)} custom-call(bf16[2,128,128]{2,1,0:T(8,128)(2,1)S(1)} %get-tuple-element.5.mine), custom_call_target="tpu_custom_call" | custom-call | tf_op jit(solution)/shard_map/gather/pallas_call | solution.py:466
  63.8 0.0 copy-done.1
  63.8 0.0 copy-done.5
  63.8 6.8 %backward.1 = bf16[2,512,512]{2,1,0:T(8,128)(2,1)} custom-call(s32[1,2]{1,0:T(1,128)S(1)} %copy-done.10, s32[16,2]{1,0:T(8,128)S(1)} %copy.15.soff, bf16[16,2,128,128]{3,2,1,0:T(8,128)(2,1)S(1)} %gather.1.piece, bf16[2,512,512]{2,1,0:T(8,128)(2,1)S(1)} %copy-done.1, f32[128,128]{1,0:T(8,128)S(1)} %copy-done.5), custom_call_target="tpu_custom_call" | custom-call | tf_op jit(solution)/shard_map/backward/pallas_call | solution.py:478
Async XLA Ops:
  1.9 0.7 copy-start.11
  2.6 0.7 copy-start.12
  3.3 0.7 copy-start.10
  3.9 1.2 %copy-start = (bf16[2,512,512]{2,1,0:T(8,128)(2,1)S(1)}, bf16[2,512,512]{2,1,0:T(8,128)(2,1)}, u32[]{:S(2)}) copy-start(bf16[2,512,512]{2,1,0:T(8,128)(2,1)} %constant.12.clone.basis) | copy-start | bytes 3145732
  5.2 1.2 %copy-start.2 = (bf16[1,2,512,512]{3,2,1,0:T(8,128)(2,1)S(1)}, bf16[1,2,512,512]{3,2,1,0:T(8,128)(2,1)}, u32[]{:S(2)}) copy-start(bf16[1,2,512,512]{3,2,1,0:T(8,128)(2,1)} %param.13) | copy-start | bytes 3145732
  6.4 0.8 %copy-start.4 = (f32[128,128]{1,0:T(8,128)S(1)}, f32[128,128]{1,0:T(8,128)}, u32[]{:S(2)}) copy-start(f32[128,128]{1,0:T(8,128)} %constant.15.clone.taper) | copy-start | bytes 196612
  7.2 22.2 %copy-start.6 = (f32[512,128]{1,0:T(8,128)S(1)}, f32[512,128]{1,0:T(8,128)}, u32[]{:S(2)}) copy-start(f32[512,128]{1,0:T(8,128)} %constant.17.clone.ker_t) | copy-start | bytes 786436
  7.2 22.2 %copy-start.7 = (bf16[2,128,512]{2,1,0:T(8,128)(2,1)S(1)}, bf16[2,128,512]{2,1,0:T(8,128)(2,1)}, u32[]{:S(2)}) copy-start(bf16[2,128,512]{2,1,0:T(8,128)(2,1)} %constant.14.clone.pad_t) | copy-start | bytes 786436
  7.2 22.2 %copy-start.8 = (bf16[2,512,128]{2,1,0:T(8,128)(2,1)S(1)}, bf16[2,512,128]{2,1,0:T(8,128)(2,1)}, u32[]{:S(2)}) copy-start(bf16[2,512,128]{2,1,0:T(8,128)(2,1)} %constant.13.clone.pad) | copy-start | bytes 786436
  7.2 22.2 %copy-start.9 = (f32[128,384]{1,0:T(8,128)S(1)}, f32[128,384]{1,0:T(8,128)}, u32[]{:S(2)}) copy-start(f32[128,384]{1,0:T(8,128)} %constant.16.clone.ker) | copy-start | bytes 589828
  13.2 16.2 %copy-start.3 = (bf16[16,2,128,128]{3,2,1,0:T(8,128)(2,1)S(1)}, bf16[16,2,128,128]{3,2,1,0:T(8,128)(2,1)}, u32[]{:S(2)}) copy-start(bf16[16,2,128,128]{3,2,1,0:T(8,128)(2,1)} %observed.1) | copy-start | bytes 3145732
  36.5 27.3 %copy-start.1 = (bf16[2,512,512]{2,1,0:T(8,128)(2,1)S(1)}, bf16[2,512,512]{2,1,0:T(8,128)(2,1)}, u32[]{:S(2)}) copy-start(bf16[2,512,512]{2,1,0:T(8,128)(2,1)} %constant.12.clone.basis) | copy-start | bytes 3145732
  36.5 27.3 %copy-start.5 = (f32[128,128]{1,0:T(8,128)S(1)}, f32[128,128]{1,0:T(8,128)}, u32[]{:S(2)}) copy-start(f32[128,128]{1,0:T(8,128)} %constant.15.clone.taper) | copy-start | bytes 196612
